TPU v7x, 32 devices: a whole 2x2x4 slice. The times are simulated.
32 devices in a mesh: gx: 8 (over z, core), gy: 4 (over y, x).
Axes of the slice: x: 2, y: 2, z: 4, core: 2. Of those that a mesh axis runs over, the one named last changes fastest.
Arguments:
- water_depth: float32 [1024, 1536], P('gx', 'gy'), may hold values from 0.3 to 3
- bed_level: float32 [1024, 1536], P('gx', 'gy'), may hold values from 0 to 2
- east_flow: float32 [1024, 1536], P('gx', 'gy'), may hold values from -4 to 4
- south_flow: float32 [1024, 1536], P('gx', 'gy'), may hold values from -4 to 4
- roughness_class: int32 [1024, 1536], P('gx', 'gy'), may hold values from 0 to 7
- wet_mask: int32 [1024, 1536], P('gx', 'gy'), may hold values 0 or 1
- soil_store: float32 [8, 1536, 128], P('gx', 'gy'), may hold values from 0.05 to 0.95
- rainfall: float32 [8, 1536, 128], P('gx', 'gy'), may hold values from 0 to 0.5
- tile_column: int32 [8, 1536, 1], P('gx', 'gy'), may hold values from 0 to 3; in each aligned block of 384 rows (0 to 383, 384 to 767, ..., all dimensions but the last counted through in order) at most 192 rows name the same one
- tile_block: int32 [8, 1536], P('gx', 'gy'), may hold values from 0 to 383
Outputs:
- new_depth: float32 [1024, 1536], P('gx', 'gy')
- new_east_flow: float32 [1024, 1536], P('gx', 'gy')
- new_south_flow: float32 [1024, 1536], P('gx', 'gy')
- new_soil: float32 [8, 1536, 128], P('gx', 'gy')
Inputs may be any that keep to these rules, and one draw needn't show every extreme that they name: `tile_column`: among the 384 land blocks of one device, at most 192 name the same tile column; in some device some tile column is named by exactly 192 of them. `tile_block`: several land blocks may name the same block of a tile; some blocks are named by none.
All inputs are finite; a program needn't handle non-finite values. No bound on the sum of `wet_mask` on one device may be relied on, other than what follows from the above.
Results may differ from a plain program's by a relative error of at most 0.00002.
Values sent between devices are 32-bit elements; how exact they have to be, the bound alone decides.
A program may use at most 64 MiB of HBM per device.

v0:
```python
import functools

import jax
import jax.numpy as jnp
from jax import lax
from jax.experimental import pallas as pl
from jax.experimental.pallas import tpu as pltpu
from jax.sharding import PartitionSpec as P

SUB = 4
GRAVITY = 9.81
TIME_STEP = 1.0
CELL_WIDTH = 30.0
DEPTH_FLOOR = 0.3
INFIL_RATE = 0.5
MANNING = (0.02, 0.03, 0.035, 0.045, 0.06, 0.08, 0.1, 0.15)
LANES = 128
EDGE = 8
MESH = pl.DeviceIdType.MESH
AROUND = ((-1, -1), (-1, 0), (-1, 1), (0, -1), (0, 1), (1, -1), (1, 0), (1, 1))
NW, N, NE, W, E, SW, S, SE = range(8)


def split(x):
    a = x.astype(jnp.bfloat16)
    b = (x - a.astype(jnp.float32)).astype(jnp.bfloat16)
    return jnp.concatenate([a, b], axis=1)


def pick(mask, x):
    x = x if x.dtype == jnp.bfloat16 else split(x)
    y = jnp.dot(mask, x, preferred_element_type=jnp.float32)
    return y[:, :LANES] + y[:, LANES:]


def flip(i, k, n):
    if n & (n - 1):
        return None
    both, bit = 0, 1
    while bit < n:
        if k & bit:
            both = both + bit * lax.rem(i // bit, 2)
        bit *= 2
    return i + k - 2 * both


def offsets(n):
    return sorted(range(1, n), key=lambda k: bin(k).count("1"))


def east_of(x):
    return pltpu.roll(x, x.shape[1] - 1, 1)


def south_of(x):
    return pltpu.roll(x, x.shape[0] - 1, 0)


def face(eta, eta_next, base, coef, q):
    depth = jnp.maximum(eta, eta_next) - base
    driving = (GRAVITY * TIME_STEP / CELL_WIDTH) * jnp.maximum(depth, 0.0) * (eta_next - eta)
    power = jnp.exp2(jnp.log2(jnp.maximum(depth, DEPTH_FLOOR)) * (-7.0 / 3.0))
    damping = 1.0 + coef * jnp.abs(q) * power
    return jnp.where(coef > 0.0, (q - driving) / damping, 0.0)


def kernel(
    nx, ny, cap,
    depth_in, bed_in, east_in, south_in, rough_in, wet_in, soil_in, rain_in, col_in, blk_in,
    h, qe, qs, newsoil,
    bed, fric, rough, wet, land_in, index,
    base_e, base_s, coef_e, coef_s,
    give, take, give_idx, take_idx, give_lev, take_lev,
    st_rows, st_cols, st_corner, st_in_rows, st_in_cols, st_in_corner,
    h_rows, h_cols, h_in_rows, h_in_cols, h_in_corner,
    place, place_t, where_to, where_to_t, span,
    in_sem, give_r, lev_r, data_s, idx_s, idx_r, st_s, st_r, hs_s, hs_r,
):
    gx, gy = lax.axis_index("gx"), lax.axis_index("gy")
    tr, tc = rough.shape
    land = land_in.shape[1]
    chunks = tc // LANES

    inner = (pl.ds(0, tr), pl.ds(0, tc))
    loads = [
        pltpu.make_async_copy(src, dst, in_sem.at[i])
        for i, src, dst in [
            (0, col_in, index.at[0]), (0, blk_in, index.at[1]),
            (1, soil_in, land_in.at[0]), (1, rain_in, land_in.at[1]),
            (2, rough_in, rough), (2, wet_in, wet), (2, bed_in, bed.at[inner]),
            (2, east_in, qe.at[inner]), (2, south_in, qs.at[inner]),
            (3, depth_in, h.at[inner]),
        ]
    ]
    for c in loads:
        c.start()

    def settle(sem, tiles):
        ref = span.at[pl.ds(0, tiles)]
        pltpu.make_async_copy(ref, ref, sem).wait()

    def there(k):
        dx, dy = AROUND[k]
        x, y = gx + dx, gy + dy
        return (x >= 0) & (x < nx) & (y >= 0) & (y < ny)

    barrier = pltpu.get_barrier_semaphore()
    for k in range(1, ny):
        pl.semaphore_signal(
            barrier, inc=1, device_id=(gx, lax.rem(gy + k, ny)), device_id_type=MESH
        )
    total = ny - 1
    for k in (NW, N, NE, SW, S, SE):
        dx, dy = AROUND[k]

        @pl.when(there(k))
        def _(dx=dx, dy=dy):
            pl.semaphore_signal(barrier, inc=1, device_id=(gx + dx, gy + dy), device_id_type=MESH)

        total = total + there(k).astype(jnp.int32)

    for k, ref in ((N, (st_in_rows, h_in_rows)), (S, (st_in_rows, h_in_rows))):
        @pl.when(jnp.logical_not(there(k)))
        def _(k=k, ref=ref):
            for r in ref:
                r[int(k == S)] = jnp.zeros(r.shape[1:], r.dtype)
    for k, ref in ((W, (st_in_cols, h_in_cols)), (E, (st_in_cols, h_in_cols))):
        @pl.when(jnp.logical_not(there(k)))
        def _(k=k, ref=ref):
            for r in ref:
                r[int(k == E)] = jnp.zeros(r.shape[1:], r.dtype)
    for n, k in enumerate((NW, NE, SW, SE)):
        @pl.when(jnp.logical_not(there(k)))
        def _(n=n):
            for r in (st_in_corner, h_in_corner):
                r[n] = jnp.zeros(r.shape[1:], r.dtype)

    def to_peer(k):
        if k == 0:
            return gy
        peer = flip(gy, k, ny)
        return lax.rem(gy + k, ny) if peer is None else peer

    def from_peer(k):
        peer = flip(gy, k, ny)
        return lax.rem(gy + ny - k, ny) if peer is None else peer

    def send(src, dst, ss, rs, peer):
        pltpu.make_async_remote_copy(
            src_ref=src, dst_ref=dst, send_sem=ss, recv_sem=rs,
            device_id=(gx, peer), device_id_type=MESH,
        ).start()

    def arrive(dst, rs):
        pltpu.make_async_copy(dst, dst, rs).wait()

    pltpu.make_async_copy(index, index, in_sem.at[0]).wait()
    column = index[0]
    groups = max(EDGE, ny)
    is_col = lax.broadcasted_iota(jnp.int32, (groups, land), 0) == column
    before = lax.broadcasted_iota(jnp.int32, (land, land), 0) < lax.broadcasted_iota(
        jnp.int32, (land, land), 1
    )
    rank = jnp.dot(
        is_col.astype(jnp.float32).astype(jnp.bfloat16),
        before.astype(jnp.float32).astype(jnp.bfloat16),
        preferred_element_type=jnp.float32,
    )
    rank = jnp.sum(jnp.where(is_col, rank, 0.0), axis=0, keepdims=True)
    slot = column.astype(jnp.float32) * cap + rank

    block = index[1].astype(jnp.float32)
    row = jnp.floor((block + 0.5) * (1.0 / chunks))
    chunk = block - row * chunks
    line = lax.broadcasted_iota(jnp.int32, (EDGE, land), 0)
    code = jnp.where(line == 0, row + 1.0, jnp.where(line == 1, chunk, 0.0))
    code = code.astype(jnp.bfloat16)
    seat = lax.broadcasted_iota(jnp.int32, (cap, land), 0).astype(jnp.float32)

    pltpu.make_async_copy(land_in, land_in, in_sem.at[1]).wait()
    runoff = split(land_in[1] * land_in[0] * land_in[0])

    def pack(k):
        hit = (seat == slot - (to_peer(k) * cap).astype(jnp.float32)).astype(jnp.float32)
        mask = hit.astype(jnp.bfloat16)
        place[k] = mask
        owner = lax.dot_general(
            code, mask, (((1,), (1,)), ((), ())), preferred_element_type=jnp.float32
        )
        give_idx[k] = owner[1:2] * tr + owner[0:1] - 1.0
        give[k] = pick(mask, runoff)

    for n, k in enumerate(offsets(ny)):
        pack(k)
        if n == 0:
            pl.semaphore_wait(barrier, total)
        send(give_idx.at[k], take_idx.at[k], idx_s, idx_r, to_peer(k))
        send(give.at[k], take.at[k], data_s, give_r.at[k - 1], to_peer(k))
    pack(0)
    take_idx[0] = give_idx[0]

    settle(in_sem.at[2], 5 * tr * tc // (EDGE * LANES))
    kind = rough[...]
    f = jnp.zeros((tr, tc), jnp.float32)
    for i, coefficient in enumerate(MANNING):
        f = jnp.where(kind == i, coefficient * coefficient, f)
    fric[inner] = jnp.where(wet[...] > 0, f, -1.0)
    lane_low = lax.broadcasted_iota(jnp.int32, (tr, LANES), 1) < LANES // 2
    low8 = lane_low[:EDGE]
    sub_low = lax.broadcasted_iota(jnp.int32, (EDGE, 1), 0) < EDGE // 2
    half_turn = lambda x: pltpu.roll(x, EDGE // 2, 0)
    first, last = pl.ds(0, LANES), pl.ds(tc - LANES, LANES)

    def ends_of(ref):
        ends = jnp.where(lane_low, ref[0:tr, 0:LANES], ref[0:tr, tc - LANES : tc]).T
        return ends[0:EDGE], ends[LANES - EDGE :]

    pairs = ((bed, fric), (qe, qs))
    for i, (a, b) in enumerate(pairs):
        st_rows[0, i] = jnp.where(sub_low, a[0:EDGE, 0:tc], half_turn(b[0:EDGE, 0:tc]))
        st_rows[1, i] = jnp.where(
            sub_low, half_turn(b[tr - EDGE : tr, 0:tc]), a[tr - EDGE : tr, 0:tc]
        )
        (aw, ae), (bw, be) = ends_of(a), ends_of(b)
        st_cols[0, i] = jnp.where(sub_low, aw, half_turn(bw))
        st_cols[1, i] = jnp.where(sub_low, half_turn(be), ae)
    for dx in range(2):
        x, y = st_rows[dx, 0, :, first], st_rows[dx, 1, :, first]
        st_corner[dx, 0] = jnp.where(low8, x, pltpu.roll(y, LANES // 2, 1))
        x, y = st_rows[dx, 0, :, last], st_rows[dx, 1, :, last]
        st_corner[dx, 1] = jnp.where(low8, pltpu.roll(y, LANES // 2, 1), x)

    def edges(piece, tiles, ss, rs):
        def start():
            for k in (NW, NE, SW, SE, W, E, N, S):
                @pl.when(there(k))
                def _(k=k):
                    dx, dy = AROUND[k]
                    src, dst = piece(k)
                    pltpu.make_async_remote_copy(
                        src_ref=src, dst_ref=dst, send_sem=ss, recv_sem=rs,
                        device_id=(gx + dx, gy + dy), device_id_type=MESH,
                    ).start()

        def wait(sem):
            up = (gx > 0).astype(jnp.int32) + (gx < nx - 1).astype(jnp.int32)
            side = (gy > 0).astype(jnp.int32) + (gy < ny - 1).astype(jnp.int32)
            for r in range(3):
                for c in range(3):
                    n = r * tiles[0] + c * tiles[1] + r * c * tiles[2]
                    if n:
                        @pl.when((up == r) & (side == c))
                        def _(n=n):
                            settle(sem, n)

        return start, lambda: wait(rs), lambda: wait(ss)

    corner_at = {NW: 3, NE: 2, SW: 1, SE: 0}

    def st_piece(k):
        dx, dy = AROUND[k]
        if dy == 0:
            return st_rows.at[int(dx > 0)], st_in_rows.at[int(dx < 0)]
        if dx == 0:
            return st_cols.at[int(dy > 0)], st_in_cols.at[int(dy < 0)]
        return st_corner.at[int(dx > 0), int(dy > 0)], st_in_corner.at[corner_at[k]]

    def h_piece(k):
        dx, dy = AROUND[k]
        if dy == 0:
            return h_rows.at[int(dx > 0)], h_in_rows.at[int(dx < 0)]
        if dx == 0:
            return h_cols.at[int(dy > 0)], h_in_cols.at[int(dy < 0)]
        side = last if dy > 0 else first
        return h_rows.at[int(dx > 0), :, side], h_in_corner.at[corner_at[k]]

    st_start, st_wait, st_done = edges(
        st_piece, (2 * chunks, 2 * (tr // LANES), 1), st_s, st_r
    )
    h_start, h_wait, h_done = edges(h_piece, (chunks, tr // LANES, 1), hs_s, hs_r)
    st_start()

    for d in range(ny):
        place_t[d] = place[d].astype(jnp.float32).T.astype(jnp.bfloat16)

    settle_idx = take_idx.at[pl.ds(1, ny - 1)]
    if ny > 1:
        arrive(settle_idx, idx_r)
    line = lax.broadcasted_iota(jnp.int32, (land, cap), 0).astype(jnp.float32)
    for d in range(ny):
        target = (line == take_idx[d]).astype(jnp.float32)
        where_to[d] = target.astype(jnp.bfloat16)
        where_to_t[d] = target.T.astype(jnp.bfloat16)

    pltpu.make_async_copy(depth_in, h.at[inner], in_sem.at[3]).wait()
    inflow = pick(where_to[0], give[0])
    for k in offsets(ny):
        arrive(take.at[k], give_r.at[k - 1])
        inflow = inflow + pick(where_to[k], take[k])
    for c in range(chunks):
        at = (pl.ds(0, tr), pl.ds(c * LANES, LANES))
        h[at] = h[at] + inflow[c * tr : (c + 1) * tr]

    h_rows[0] = h[0:EDGE, 0:tc]
    h_rows[1] = h[tr - EDGE : tr, 0:tc]
    h_cols[0], h_cols[1] = ends_of(h)
    h_start()

    def sides(west, east):
        side = jnp.concatenate(
            [east, jnp.zeros((LANES - 2 * EDGE, tr), jnp.float32), west], axis=0
        )
        return side.T

    def quarter(nw, ne, sw, se):
        return jnp.where(low8, jnp.where(sub_low, se, ne), jnp.where(sub_low, sw, nw))

    st_wait()
    corners = [st_in_corner[n] for n in range(4)]
    nw, ne, sw, se = corners
    for i, (a, b) in enumerate(pairs):
        up, down = st_in_rows[0, i], st_in_rows[1, i]
        a[tr : tr + EDGE, 0:tc] = jnp.where(sub_low, down, up)
        b[tr : tr + EDGE, 0:tc] = half_turn(jnp.where(sub_low, up, down))
        west, east = st_in_cols[0, i], st_in_cols[1, i]
        a[0:tr, tc : tc + LANES] = sides(west, east)
        b[0:tr, tc : tc + LANES] = sides(half_turn(west), half_turn(east))
        if i == 0:
            ca, cb = quarter(nw, ne, sw, se), half_turn(quarter(sw, se, nw, ne))
        else:
            ca = pltpu.roll(quarter(ne, nw, se, sw), LANES // 2, 1)
            cb = half_turn(pltpu.roll(quarter(se, sw, ne, nw), LANES // 2, 1))
        a[tr : tr + EDGE, tc : tc + LANES] = ca
        b[tr : tr + EDGE, tc : tc + LANES] = cb
    b, fr = bed[...], fric[...]
    b_e, f_e, b_s, f_s = east_of(b), east_of(fr), south_of(b), south_of(fr)
    half = 0.5 * GRAVITY * TIME_STEP
    base_e[...] = jnp.maximum(b, b_e)
    base_s[...] = jnp.maximum(b, b_s)
    coef_e[...] = jnp.where((fr > 0.0) & (f_e > 0.0), half * (fr + f_e), -1.0)
    coef_s[...] = jnp.where((fr > 0.0) & (f_s > 0.0), half * (fr + f_s), -1.0)

    h_wait()
    h[tr : tr + EDGE, 0:tc] = jnp.where(sub_low, h_in_rows[1], h_in_rows[0])
    h[0:tr, tc : tc + LANES] = sides(h_in_cols[0], h_in_cols[1])
    h[tr : tr + EDGE, tc : tc + LANES] = quarter(*[h_in_corner[n] for n in range(4)])

    for step in range(SUB):
        eta = h[...] + bed[...]
        e = face(eta, east_of(eta), base_e[...], coef_e[...], qe[...])
        s = face(eta, south_of(eta), base_s[...], coef_s[...], qs[...])
        qe[...] = e
        qs[...] = s
        h[...] = h[...] + (TIME_STEP / CELL_WIDTH) * (
            pltpu.roll(e, 1, 1) - e + pltpu.roll(s, 1, 0) - s
        )

    blocks = split(jnp.concatenate(
        [h[0:tr, c * LANES : (c + 1) * LANES] for c in range(chunks)], axis=0
    ))
    for k in offsets(ny):
        give_lev[k] = pick(where_to_t[k], blocks)
        send(give_lev.at[k], take_lev.at[k], data_s, lev_r.at[k - 1], from_peer(k))
    mine = pick(place_t[0], pick(where_to_t[0], blocks))
    for k in offsets(ny):
        arrive(take_lev.at[k], lev_r.at[k - 1])
        mine = mine + pick(place_t[k], take_lev[k])
    store, rain = land_in[0], land_in[1]
    runoff = rain * store * store
    newsoil[...] = (
        store + rain - runoff + INFIL_RATE * (1.0 - store) * (1.0 - jnp.exp(-mine))
    )
    if ny > 1:
        arrive(settle_idx, idx_s)
        settle(data_s, 2 * (ny - 1) * cap // EDGE)
    st_done()
    h_done()


def write_out(h, qe, qs, newsoil, depth_out, east_out, south_out, soil_out, sem):
    tr, tc = depth_out.shape
    inner = (pl.ds(0, tr), pl.ds(0, tc))
    copies = [
        pltpu.make_async_copy(src, dst, sem.at[i])
        for i, (src, dst) in enumerate(
            [
                (h.at[inner], depth_out), (qe.at[inner], east_out),
                (qs.at[inner], south_out), (newsoil, soil_out),
            ]
        )
    ]
    for c in copies:
        c.start()
    for c in copies:
        c.wait()


def local(depth, bed, east, south, rough, wet, soil, rain, column, block):
    nx, ny = lax.axis_size("gx"), lax.axis_size("gy")
    tr, tc = depth.shape
    land = soil.shape[1]
    cap = 2 * land // ny
    grid = (tr + EDGE, tc + LANES)
    f32, bf16, i32 = jnp.float32, jnp.bfloat16, jnp.int32
    v = pltpu.VMEM
    dma = pltpu.SemaphoreType.DMA
    peers = max(1, ny - 1)

    def edge_bufs(k):
        return [v((2, *k, EDGE, tc), f32), v((2, *k, EDGE, tr), f32)]

    corners = v((2, 2, EDGE, LANES), f32)
    in_corners = v((4, EDGE, LANES), f32)
    span = max(5 * tr * tc, 2 * peers * cap * LANES, 4 * EDGE * (2 * tc + 2 * tr + 4 * LANES))
    any_ = pl.BlockSpec(memory_space=pltpu.MemorySpace.HBM)
    vmem = pl.BlockSpec(memory_space=pltpu.VMEM)
    shape = jax.ShapeDtypeStruct
    out = pl.pallas_call(
        functools.partial(kernel, nx, ny, cap),
        out_shape=[shape(grid, f32)] * 3 + [shape((land, LANES), f32)],
        in_specs=[any_] * 10,
        out_specs=[vmem] * 4,
        scratch_shapes=[v(grid, f32)] * 2
        + [v((tr, tc), i32)] * 2
        + [v((2, land, LANES), f32), v((2, 1, land), i32)]
        + [v(grid, f32)] * 4
        + [v((ny, cap, LANES), f32)] * 2
        + [v((ny, 1, cap), f32)] * 2
        + [v((ny, cap, LANES), f32)] * 2
        + edge_bufs((2,)) + [corners] + edge_bufs((2,)) + [in_corners]
        + edge_bufs(()) + edge_bufs(()) + [in_corners]
        + [v((ny, cap, land), bf16), v((ny, land, cap), bf16)]
        + [v((ny, land, cap), bf16), v((ny, cap, land), bf16)]
        + [v((span // (EDGE * LANES), EDGE, LANES), f32)]
        + [dma((4,))]
        + [dma((peers,))] * 2
        + [dma] * 7,
        compiler_params=pltpu.CompilerParams(collective_id=0, has_side_effects=True, vmem_limit_bytes=24 << 20
        ),
    )(
        *(
            pltpu.with_memory_space_constraint(x, pltpu.MemorySpace.HBM)
            for x in (
                depth, bed, east, south, rough, wet, soil[0], rain[0],
                column.reshape(1, land), block,
            )
        )
    )
    out = pl.pallas_call(
        write_out,
        out_shape=[shape((tr, tc), f32)] * 3 + [shape((land, LANES), f32)],
        in_specs=[vmem] * 4,
        out_specs=[any_] * 4,
        scratch_shapes=[dma((4,))],
        compiler_params=pltpu.CompilerParams(vmem_limit_bytes=8 << 20),
    )(*out)
    return out[0], out[1], out[2], out[3][None]


def solution(mesh):
    grid = P("gx", "gy")
    blocks = P("gx", "gy", None)
    return jax.shard_map(
        local, mesh=mesh,
        in_specs=(grid,) * 6 + (blocks,) * 3 + (grid,),
        out_specs=(grid,) * 3 + (blocks,),
        check_vma=False,
    )
```

profile of v0, /device:TPU:0, one launch (start us, length us, event | category | flops | bytes accessed | tf_op | source)
XLA Modules:
  0.0 25.1 jit_solution(4263623095320712911)
XLA Ops:
  0.6 23.5 %shard_map.129 = (f32[136,512]{1,0:T(8,128)S(1)}, f32[136,512]{1,0:T(8,128)S(1)}, f32[136,512]{1,0:T(8,128)S(1)}, f32[384,128]{1,0:T(8,128)S(1)}) custom-call(f32[128,384]{1,0:T(8,128)} %depth_in.1, f32[128,384]{1,0:T(8,128)} %bed_in.1, f32[128,384]{1,0:T(8,128)} %east_in.1, f32[128,384]{1,0:T(8,128)} %south_in.1, s32[128,384]{1,0:T(8,128)} %rough_in.1, ...), custom_call_target="tpu_custom_call" | custom-call | tf_op jit(solution)/shard_map/pallas_call | solution.py:418
  24.2 0.9 %shard_map.130 = (f32[128,384]{1,0:T(8,128)}, f32[128,384]{1,0:T(8,128)}, f32[128,384]{1,0:T(8,128)}, f32[384,128]{1,0:T(8,128)}) custom-call(f32[136,512]{1,0:T(8,128)S(1)} %get-tuple-element.12.h, f32[136,512]{1,0:T(8,128)S(1)} %get-tuple-element.13.qe, f32[136,512]{1,0:T(8,128)S(1)} %get-tuple-element.14.qs, f32[384,128]{1,0:T(8,128)S(1)} %get-tuple-element.15.newsoil), custom_call_target="tpu_custom_call" | custom-call | tf_op jit(solution)/shard_map/pallas_call | solution.py:449
where the time goes:
time: 25.2 us; the launch traced here: 25.1 us
  Pallas kernels  24.4 us (97%)
  between operations  0.64 us (3%)
    pallas_call x1, Pallas kernels, local(): pl.pallas_call(functools.partial(kernel, nx, ny, cap), out_shape=[shape(g...  23.5 us
    pallas_call x1, Pallas kernels, local(): pl.pallas_call(write_out, out_shape=[shape((tr, tc), f32)] * 3 + [shape((...  0.91 us

commit v1 on v0

--- a/solution.py
+++ b/solution.py
@@ -69,7 +69,7 @@
     depth_in, bed_in, east_in, south_in, rough_in, wet_in, soil_in, rain_in, col_in, blk_in,
     h, qe, qs, newsoil,
     bed, fric, rough, wet, land_in, index,
-    base_e, base_s, coef_e, coef_s,
+    tile_face, rim, rim_face, flank, flank_face,
     give, take, give_idx, take_idx, give_lev, take_lev,
     st_rows, st_cols, st_corner, st_in_rows, st_in_cols, st_in_corner,
     h_rows, h_cols, h_in_rows, h_in_cols, h_in_corner,
@@ -81,15 +81,13 @@
     land = land_in.shape[1]
     chunks = tc // LANES
 
-    inner = (pl.ds(0, tr), pl.ds(0, tc))
     loads = [
         pltpu.make_async_copy(src, dst, in_sem.at[i])
         for i, src, dst in [
             (0, col_in, index.at[0]), (0, blk_in, index.at[1]),
             (1, soil_in, land_in.at[0]), (1, rain_in, land_in.at[1]),
-            (2, rough_in, rough), (2, wet_in, wet), (2, bed_in, bed.at[inner]),
-            (2, east_in, qe.at[inner]), (2, south_in, qs.at[inner]),
-            (3, depth_in, h.at[inner]),
+            (2, rough_in, rough), (2, wet_in, wet), (2, bed_in, bed),
+            (2, east_in, qe), (2, south_in, qs), (3, depth_in, h),
         ]
     ]
     for c in loads:
@@ -204,7 +202,7 @@
     f = jnp.zeros((tr, tc), jnp.float32)
     for i, coefficient in enumerate(MANNING):
         f = jnp.where(kind == i, coefficient * coefficient, f)
-    fric[inner] = jnp.where(wet[...] > 0, f, -1.0)
+    fric[...] = jnp.where(wet[...] > 0, f, -1.0)
     lane_low = lax.broadcasted_iota(jnp.int32, (tr, LANES), 1) < LANES // 2
     low8 = lane_low[:EDGE]
     sub_low = lax.broadcasted_iota(jnp.int32, (EDGE, 1), 0) < EDGE // 2
@@ -280,6 +278,39 @@
     h_start, h_wait, h_done = edges(h_piece, (chunks, tr // LANES, 1), hs_s, hs_r)
     st_start()
 
+    lane = lax.broadcasted_iota(jnp.int32, (tr, LANES), 1)
+    own = lane < LANES // 2
+
+    def keep(x, i):
+        rim[i, 0:EDGE] = x[tr - EDGE : tr, 0:tc]
+        rim[i, 2 * EDGE : 3 * EDGE] = x[0:EDGE, 0:tc]
+        flank[i, 0:tr] = jnp.where(
+            lane < LANES // 4,
+            x[0:tr, 0:LANES],
+            pltpu.roll(x[0:tr, tc - LANES : tc], LANES // 2, 1),
+        )
+
+    def faces(b, fr, out):
+        b_e, f_e, b_s, f_s = east_of(b), east_of(fr), south_of(b), south_of(fr)
+        half = 0.5 * GRAVITY * TIME_STEP
+        out[0] = jnp.maximum(b, b_e)
+        out[1] = jnp.maximum(b, b_s)
+        out[2] = jnp.where((fr > 0.0) & (f_e > 0.0), half * (fr + f_e), -1.0)
+        out[3] = jnp.where((fr > 0.0) & (f_s > 0.0), half * (fr + f_s), -1.0)
+
+    def substep(depth, b, e, s, out):
+        eta = depth + b
+        e = face(eta, east_of(eta), out[0], out[2], e)
+        s = face(eta, south_of(eta), out[1], out[3], s)
+        depth = depth + (TIME_STEP / CELL_WIDTH) * (
+            pltpu.roll(e, 1, 1) - e + pltpu.roll(s, 1, 0) - s
+        )
+        return depth, e, s
+
+    for i, x in enumerate((bed, fric, qe, qs)):
+        keep(x, i)
+    faces(bed[...], fric[...], tile_face)
+
     for d in range(ny):
         place_t[d] = place[d].astype(jnp.float32).T.astype(jnp.bfloat16)
 
@@ -292,7 +323,7 @@
         where_to[d] = target.astype(jnp.bfloat16)
         where_to_t[d] = target.T.astype(jnp.bfloat16)
 
-    pltpu.make_async_copy(depth_in, h.at[inner], in_sem.at[3]).wait()
+    pltpu.make_async_copy(depth_in, h, in_sem.at[3]).wait()
     inflow = pick(where_to[0], give[0])
     for k in offsets(ny):
         arrive(take.at[k], give_r.at[k - 1])
@@ -305,54 +336,63 @@
     h_rows[1] = h[tr - EDGE : tr, 0:tc]
     h_cols[0], h_cols[1] = ends_of(h)
     h_start()
-
-    def sides(west, east):
-        side = jnp.concatenate(
-            [east, jnp.zeros((LANES - 2 * EDGE, tr), jnp.float32), west], axis=0
-        )
-        return side.T
-
-    def quarter(nw, ne, sw, se):
-        return jnp.where(low8, jnp.where(sub_low, se, ne), jnp.where(sub_low, sw, nw))
+    keep(h, 4)
+
+    for step in range(SUB):
+        h[...], qe[...], qs[...] = substep(h[...], bed[...], qe[...], qs[...], tile_face)
+
+    gap = jnp.zeros((LANES // 2 - 2 * EDGE, tr), jnp.float32)
+    half_gap = jnp.zeros((LANES // 2, tr), jnp.float32)
+    lane8 = lane[:EDGE]
+
+    def wrap(i, halo, west, east, corner_w, corner_e):
+        side = jnp.concatenate([half_gap, east, gap, west], axis=0)
+        rim[i, EDGE : 2 * EDGE] = halo
+        flank[i, 0:tr] = jnp.where(own, flank[i, 0:tr], side.T)
+        corner = jnp.where(lane8 < 3 * LANES // 4, corner_e, corner_w)
+        far = pltpu.roll(halo[:, tc - LANES :], LANES // 2, 1)
+        line = jnp.where(lane8 < LANES // 4, halo[:, :LANES], far)
+        flank[i, tr : tr + EDGE] = jnp.where(low8, line, corner)
+
+    def turn(x):
+        return pltpu.roll(x, LANES // 2, 1)
 
     st_wait()
-    corners = [st_in_corner[n] for n in range(4)]
-    nw, ne, sw, se = corners
-    for i, (a, b) in enumerate(pairs):
+    nw, ne, sw, se = [st_in_corner[n] for n in range(4)]
+    west_a, west_b = jnp.where(sub_low, sw, nw), half_turn(jnp.where(sub_low, nw, sw))
+    east_a, east_b = jnp.where(sub_low, se, ne), half_turn(jnp.where(sub_low, ne, se))
+    for i in range(2):
         up, down = st_in_rows[0, i], st_in_rows[1, i]
-        a[tr : tr + EDGE, 0:tc] = jnp.where(sub_low, down, up)
-        b[tr : tr + EDGE, 0:tc] = half_turn(jnp.where(sub_low, up, down))
         west, east = st_in_cols[0, i], st_in_cols[1, i]
-        a[0:tr, tc : tc + LANES] = sides(west, east)
-        b[0:tr, tc : tc + LANES] = sides(half_turn(west), half_turn(east))
-        if i == 0:
-            ca, cb = quarter(nw, ne, sw, se), half_turn(quarter(sw, se, nw, ne))
-        else:
-            ca = pltpu.roll(quarter(ne, nw, se, sw), LANES // 2, 1)
-            cb = half_turn(pltpu.roll(quarter(se, sw, ne, nw), LANES // 2, 1))
-        a[tr : tr + EDGE, tc : tc + LANES] = ca
-        b[tr : tr + EDGE, tc : tc + LANES] = cb
-    b, fr = bed[...], fric[...]
-    b_e, f_e, b_s, f_s = east_of(b), east_of(fr), south_of(b), south_of(fr)
-    half = 0.5 * GRAVITY * TIME_STEP
-    base_e[...] = jnp.maximum(b, b_e)
-    base_s[...] = jnp.maximum(b, b_s)
-    coef_e[...] = jnp.where((fr > 0.0) & (f_e > 0.0), half * (fr + f_e), -1.0)
-    coef_s[...] = jnp.where((fr > 0.0) & (f_s > 0.0), half * (fr + f_s), -1.0)
+        cw = (west_a, west_b) if i == 0 else (turn(west_a), turn(west_b))
+        ce = (turn(east_a), turn(east_b)) if i == 0 else (east_a, east_b)
+        wrap(2 * i, jnp.where(sub_low, down, up), west, east, cw[0], ce[0])
+        wrap(
+            2 * i + 1, half_turn(jnp.where(sub_low, up, down)), half_turn(west),
+            half_turn(east), cw[1], ce[1],
+        )
+    faces(rim[0], rim[1], rim_face)
+    faces(flank[0], flank[1], flank_face)
 
     h_wait()
-    h[tr : tr + EDGE, 0:tc] = jnp.where(sub_low, h_in_rows[1], h_in_rows[0])
-    h[0:tr, tc : tc + LANES] = sides(h_in_cols[0], h_in_cols[1])
-    h[tr : tr + EDGE, tc : tc + LANES] = quarter(*[h_in_corner[n] for n in range(4)])
+    nw, ne, sw, se = [h_in_corner[n] for n in range(4)]
+    wrap(
+        4, jnp.where(sub_low, h_in_rows[1], h_in_rows[0]), h_in_cols[0], h_in_cols[1],
+        jnp.where(sub_low, sw, nw), turn(jnp.where(sub_low, se, ne)),
+    )
 
     for step in range(SUB):
-        eta = h[...] + bed[...]
-        e = face(eta, east_of(eta), base_e[...], coef_e[...], qe[...])
-        s = face(eta, south_of(eta), base_s[...], coef_s[...], qs[...])
-        qe[...] = e
-        qs[...] = s
-        h[...] = h[...] + (TIME_STEP / CELL_WIDTH) * (
-            pltpu.roll(e, 1, 1) - e + pltpu.roll(s, 1, 0) - s
+        for x, out in ((rim, rim_face), (flank, flank_face)):
+            x[4], x[2], x[3] = substep(x[4], x[0], x[2], x[3], out)
+
+    reach = EDGE // 2
+    for i, x in ((4, h), (2, qe), (3, qs)):
+        x[0:EDGE] = jnp.where(sub_low, rim[i, 2 * EDGE : 3 * EDGE], x[0:EDGE])
+        x[tr - EDGE : tr] = jnp.where(sub_low, x[tr - EDGE : tr], rim[i, 0:EDGE])
+        edge = flank[i, 0:tr]
+        x[:, 0:LANES] = jnp.where(lane < reach, edge, x[:, 0:LANES])
+        x[:, tc - LANES : tc] = jnp.where(
+            lane >= LANES - reach, turn(edge), x[:, tc - LANES : tc]
         )
 
     blocks = split(jnp.concatenate(
@@ -378,14 +418,11 @@
 
 
 def write_out(h, qe, qs, newsoil, depth_out, east_out, south_out, soil_out, sem):
-    tr, tc = depth_out.shape
-    inner = (pl.ds(0, tr), pl.ds(0, tc))
     copies = [
         pltpu.make_async_copy(src, dst, sem.at[i])
         for i, (src, dst) in enumerate(
             [
-                (h.at[inner], depth_out), (qe.at[inner], east_out),
-                (qs.at[inner], south_out), (newsoil, soil_out),
+                (h, depth_out), (qe, east_out), (qs, south_out), (newsoil, soil_out),
             ]
         )
     ]
@@ -400,7 +437,8 @@
     tr, tc = depth.shape
     land = soil.shape[1]
     cap = 2 * land // ny
-    grid = (tr + EDGE, tc + LANES)
+    grid = (tr, tc)
+    rim, flank = (3 * EDGE, tc), (tr + EDGE, LANES)
     f32, bf16, i32 = jnp.float32, jnp.bfloat16, jnp.int32
     v = pltpu.VMEM
     dma = pltpu.SemaphoreType.DMA
@@ -423,7 +461,8 @@
         scratch_shapes=[v(grid, f32)] * 2
         + [v((tr, tc), i32)] * 2
         + [v((2, land, LANES), f32), v((2, 1, land), i32)]
-        + [v(grid, f32)] * 4
+        + [v((4, *grid), f32), v((5, *rim), f32), v((4, *rim), f32)]
+        + [v((5, *flank), f32), v((4, *flank), f32)]
         + [v((ny, cap, LANES), f32)] * 2
         + [v((ny, 1, cap), f32)] * 2
         + [v((ny, cap, LANES), f32)] * 2

time: 25.2 us -> 24.2 us (0.960)
  Pallas kernels: 24.4 us -> 23.4 us
    pallas_call x1, Pallas kernels: 23.5 us -> 22.5 us  [local(): pl.pallas_call(functools.partial(kernel, nx, ny, cap), out_shape=[shape(g...]
where the time goes in v1:
time: 24.2 us; the launch traced here: 24 us
  Pallas kernels  23.4 us (97%)
  between operations  0.64 us (3%)
    pallas_call x1, Pallas kernels, local(): pl.pallas_call(functools.partial(kernel, nx, ny, cap), out_shape=[shape(g...  22.5 us
    pallas_call x1, Pallas kernels, local(): pl.pallas_call(write_out, out_shape=[shape((tr, tc), f32)] * 3 + [shape((...  0.91 us

profile of v1, /device:TPU:0, one launch (start us, length us, event | category | flops | bytes accessed | tf_op | source)
XLA Modules:
  0.0 24.0 jit_solution(15321408374647991466)
XLA Ops:
  0.6 22.5 %shard_map.129 = (f32[128,384]{1,0:T(8,128)S(1)}, f32[128,384]{1,0:T(8,128)S(1)}, f32[128,384]{1,0:T(8,128)S(1)}, f32[384,128]{1,0:T(8,128)S(1)}) custom-call(f32[128,384]{1,0:T(8,128)} %depth_in.1, f32[128,384]{1,0:T(8,128)} %bed_in.1, f32[128,384]{1,0:T(8,128)} %east_in.1, f32[128,384]{1,0:T(8,128)} %south_in.1, s32[128,384]{1,0:T(8,128)} %rough_in.1, ...), custom_call_target="tpu_custom_call" | custom-call | tf_op jit(solution)/shard_map/pallas_call | solution.py:456
  23.1 0.9 %shard_map.130 = (f32[128,384]{1,0:T(8,128)}, f32[128,384]{1,0:T(8,128)}, f32[128,384]{1,0:T(8,128)}, f32[384,128]{1,0:T(8,128)}) custom-call(f32[128,384]{1,0:T(8,128)S(1)} %get-tuple-element.12.h, f32[128,384]{1,0:T(8,128)S(1)} %get-tuple-element.13.qe, f32[128,384]{1,0:T(8,128)S(1)} %get-tuple-element.14.qs, f32[384,128]{1,0:T(8,128)S(1)} %get-tuple-element.15.newsoil), custom_call_target="tpu_custom_call" | custom-call | tf_op jit(solution)/shard_map/pallas_call | solution.py:488

commit v2 on v1

--- a/solution.py
+++ b/solution.py
@@ -73,8 +73,8 @@
     give, take, give_idx, take_idx, give_lev, take_lev,
     st_rows, st_cols, st_corner, st_in_rows, st_in_cols, st_in_corner,
     h_rows, h_cols, h_in_rows, h_in_cols, h_in_corner,
-    place, place_t, where_to, where_to_t, span,
-    in_sem, give_r, lev_r, data_s, idx_s, idx_r, st_s, st_r, hs_s, hs_r,
+    place, place_t, where_to, where_to_t, from_row, from_col, at_end, give_edge, take_edge, span,
+    in_sem, give_r, lev_r, edge_r, data_s, idx_s, idx_r, st_s, st_r, hs_s, hs_r,
 ):
     gx, gy = lax.axis_index("gx"), lax.axis_index("gy")
     tr, tc = rough.shape
@@ -311,6 +311,27 @@
         keep(x, i)
     faces(bed[...], fric[...], tile_face)
 
+    reach = EDGE // 2
+    turn_of = jnp.zeros((1, land), jnp.float32)
+    for k in range(1, ny):
+        turn_of = jnp.where(column == to_peer(k), 1.0 * k, turn_of)
+    outer = (row < reach) | (row >= tr - reach)
+    line = jnp.where(row < reach, row, row - (tr - EDGE))
+    key = jnp.where(outer, (turn_of * chunks + chunk) * EDGE + line, -1.0)
+
+    def one_hot(rows, key):
+        line = lax.broadcasted_iota(jnp.int32, (rows, land), 0).astype(jnp.float32)
+        return (line == key).astype(jnp.float32).T.astype(jnp.bfloat16)
+
+    from_row[...] = one_hot(ny * chunks * EDGE, key)
+    head, tail = chunk == 0.0, chunk == chunks - 1.0
+    key = jnp.where((head | tail) & jnp.logical_not(outer), row, -1.0)
+    for k in range(ny):
+        from_col[k] = one_hot(tr, jnp.where(turn_of == k, key, -1.0))
+    line = lax.broadcasted_iota(jnp.int32, (LANES, land), 0)
+    ends = ((line < reach) & head) | ((line >= LANES - reach) & tail)
+    at_end[...] = ends.astype(jnp.float32).T
+
     for d in range(ny):
         place_t[d] = place[d].astype(jnp.float32).T.astype(jnp.bfloat16)
 
@@ -340,6 +361,22 @@
 
     for step in range(SUB):
         h[...], qe[...], qs[...] = substep(h[...], bed[...], qe[...], qs[...], tile_face)
+
+    high = lax.broadcasted_iota(jnp.int32, (tr, LANES), 0)
+    within = (high >= reach) & (high < tr - reach)
+    blocks = []
+    for c in range(chunks):
+        inside = within
+        if c == 0:
+            inside = inside & (lane >= reach)
+        if c == chunks - 1:
+            inside = inside & (lane < LANES - reach)
+        blocks.append(jnp.where(inside, h[:, c * LANES : (c + 1) * LANES], 0.0))
+    blocks = split(jnp.concatenate(blocks, axis=0))
+    for k in offsets(ny):
+        give_lev[k] = pick(where_to_t[k], blocks)
+        send(give_lev.at[k], take_lev.at[k], data_s, lev_r.at[k - 1], from_peer(k))
+    take_lev[0] = pick(where_to_t[0], blocks)
 
     gap = jnp.zeros((LANES // 2 - 2 * EDGE, tr), jnp.float32)
     half_gap = jnp.zeros((LANES // 2, tr), jnp.float32)
@@ -385,8 +422,7 @@
         for x, out in ((rim, rim_face), (flank, flank_face)):
             x[4], x[2], x[3] = substep(x[4], x[0], x[2], x[3], out)
 
-    reach = EDGE // 2
-    for i, x in ((4, h), (2, qe), (3, qs)):
+    def merge(i, x):
         x[0:EDGE] = jnp.where(sub_low, rim[i, 2 * EDGE : 3 * EDGE], x[0:EDGE])
         x[tr - EDGE : tr] = jnp.where(sub_low, x[tr - EDGE : tr], rim[i, 0:EDGE])
         edge = flank[i, 0:tr]
@@ -395,16 +431,31 @@
             lane >= LANES - reach, turn(edge), x[:, tc - LANES : tc]
         )
 
-    blocks = split(jnp.concatenate(
-        [h[0:tr, c * LANES : (c + 1) * LANES] for c in range(chunks)], axis=0
-    ))
+    merge(4, h)
+    give_edge[:, 0:tc] = jnp.where(sub_low, h[0:EDGE], h[tr - EDGE : tr])
+    west, east = ends_of(h)
+    give_edge[:, tc : tc + tr] = jnp.where(sub_low, west, east)
     for k in offsets(ny):
-        give_lev[k] = pick(where_to_t[k], blocks)
-        send(give_lev.at[k], take_lev.at[k], data_s, lev_r.at[k - 1], from_peer(k))
-    mine = pick(place_t[0], pick(where_to_t[0], blocks))
+        send(give_edge, take_edge.at[k], data_s, edge_r, from_peer(k))
+    take_edge[0] = give_edge[...]
+    merge(2, qe)
+    merge(3, qs)
+    mine = pick(place_t[0], take_lev[0])
     for k in offsets(ny):
         arrive(take_lev.at[k], lev_r.at[k - 1])
         mine = mine + pick(place_t[k], take_lev[k])
+    if ny > 1:
+        arrive(take_edge.at[pl.ds(1, ny - 1)], edge_r)
+    table = [
+        take_edge[k, :, c * LANES : (c + 1) * LANES] for k in range(ny) for c in range(chunks)
+    ]
+    mine = mine + pick(from_row[...], jnp.concatenate(table, axis=0))
+    blank = jnp.zeros((LANES - 2 * EDGE, tr), jnp.float32)
+    sides = jnp.zeros((land, LANES), jnp.float32)
+    for k in range(ny):
+        side = take_edge[k, :, tc : tc + tr]
+        sides = sides + pick(from_col[k], jnp.concatenate([side, blank, side], axis=0).T)
+    mine = mine + at_end[...] * sides
     store, rain = land_in[0], land_in[1]
     runoff = rain * store * store
     newsoil[...] = (
@@ -412,7 +463,7 @@
     )
     if ny > 1:
         arrive(settle_idx, idx_s)
-        settle(data_s, 2 * (ny - 1) * cap // EDGE)
+        settle(data_s, (ny - 1) * (2 * cap // EDGE + (tc + tr) // LANES))
     st_done()
     h_done()
 
@@ -449,7 +500,7 @@
 
     corners = v((2, 2, EDGE, LANES), f32)
     in_corners = v((4, EDGE, LANES), f32)
-    span = max(5 * tr * tc, 2 * peers * cap * LANES, 4 * EDGE * (2 * tc + 2 * tr + 4 * LANES))
+    span = max(5 * tr * tc, peers * (2 * cap * LANES + EDGE * (tc + tr)), 4 * EDGE * (2 * tc + 2 * tr + 4 * LANES))
     any_ = pl.BlockSpec(memory_space=pltpu.MemorySpace.HBM)
     vmem = pl.BlockSpec(memory_space=pltpu.VMEM)
     shape = jax.ShapeDtypeStruct
@@ -470,10 +521,12 @@
         + edge_bufs(()) + edge_bufs(()) + [in_corners]
         + [v((ny, cap, land), bf16), v((ny, land, cap), bf16)]
         + [v((ny, land, cap), bf16), v((ny, cap, land), bf16)]
+        + [v((land, ny * (tc // LANES) * EDGE), bf16), v((ny, land, tr), bf16), v((land, LANES), f32)]
+        + [v((EDGE, tc + tr), f32), v((ny, EDGE, tc + tr), f32)]
         + [v((span // (EDGE * LANES), EDGE, LANES), f32)]
         + [dma((4,))]
         + [dma((peers,))] * 2
-        + [dma] * 7,
+        + [dma] * 8,
         compiler_params=pltpu.CompilerParams(collective_id=0, has_side_effects=True, vmem_limit_bytes=24 << 20
         ),
     )(

time: 24.2 us -> 22.7 us (0.938)
  Pallas kernels: 23.4 us -> 21.9 us
    pallas_call x1, Pallas kernels: 22.5 us -> 21 us  [local(): pl.pallas_call(functools.partial(kernel, nx, ny, cap), out_shape=[shape(g...]
where the time goes in v2:
time: 22.7 us; the launch traced here: 22.5 us
  Pallas kernels  21.9 us (96%)
  between operations  0.64 us (3%)
    pallas_call x1, Pallas kernels, local(): pl.pallas_call(functools.partial(kernel, nx, ny, cap), out_shape=[shape(g...  21 us
    pallas_call x1, Pallas kernels, local(): pl.pallas_call(write_out, out_shape=[shape((tr, tc), f32)] * 3 + [shape((...  0.91 us

profile of v2, /device:TPU:0, one launch (start us, length us, event | category | flops | bytes accessed | tf_op | source)
XLA Modules:
  0.0 22.5 jit_solution(5622643663069460165)
XLA Ops:
  0.6 21.0 %shard_map.129 = (f32[128,384]{1,0:T(8,128)S(1)}, f32[128,384]{1,0:T(8,128)S(1)}, f32[128,384]{1,0:T(8,128)S(1)}, f32[384,128]{1,0:T(8,128)S(1)}) custom-call(f32[128,384]{1,0:T(8,128)} %depth_in.1, f32[128,384]{1,0:T(8,128)} %bed_in.1, f32[128,384]{1,0:T(8,128)} %east_in.1, f32[128,384]{1,0:T(8,128)} %south_in.1, s32[128,384]{1,0:T(8,128)} %rough_in.1, ...), custom_call_target="tpu_custom_call" | custom-call | tf_op jit(solution)/shard_map/pallas_call | solution.py:507
  21.6 0.9 %shard_map.130 = (f32[128,384]{1,0:T(8,128)}, f32[128,384]{1,0:T(8,128)}, f32[128,384]{1,0:T(8,128)}, f32[384,128]{1,0:T(8,128)}) custom-call(f32[128,384]{1,0:T(8,128)S(1)} %get-tuple-element.12.h, f32[128,384]{1,0:T(8,128)S(1)} %get-tuple-element.13.qe, f32[128,384]{1,0:T(8,128)S(1)} %get-tuple-element.14.qs, f32[384,128]{1,0:T(8,128)S(1)} %get-tuple-element.15.newsoil), custom_call_target="tpu_custom_call" | custom-call | tf_op jit(solution)/shard_map/pallas_call | solution.py:541

commit v3 on v2

--- a/solution.py
+++ b/solution.py
@@ -14,6 +14,11 @@
 DEPTH_FLOOR = 0.3
 INFIL_RATE = 0.5
 MANNING = (0.02, 0.03, 0.035, 0.045, 0.06, 0.08, 0.1, 0.15)
+POWER = -7.0 / 3.0
+STRIDE = TIME_STEP / CELL_WIDTH
+DEEP = GRAVITY * STRIDE * STRIDE
+FLOW = DEEP * STRIDE
+DRAG = 0.5 * GRAVITY * TIME_STEP * DEEP ** (-POWER) / FLOW
 LANES = 128
 EDGE = 8
 MESH = pl.DeviceIdType.MESH
@@ -56,24 +61,23 @@
     return pltpu.roll(x, x.shape[0] - 1, 0)
 
 
-def face(eta, eta_next, base, coef, q):
+def face(eta, eta_next, base, coef, closed, q):
     depth = jnp.maximum(eta, eta_next) - base
-    driving = (GRAVITY * TIME_STEP / CELL_WIDTH) * jnp.maximum(depth, 0.0) * (eta_next - eta)
-    power = jnp.exp2(jnp.log2(jnp.maximum(depth, DEPTH_FLOOR)) * (-7.0 / 3.0))
-    damping = 1.0 + coef * jnp.abs(q) * power
-    return jnp.where(coef > 0.0, (q - driving) / damping, 0.0)
+    driving = jnp.maximum(depth, 0.0) * (eta_next - eta)
+    power = jnp.exp2(jnp.log2(jnp.maximum(depth, DEEP * DEPTH_FLOOR)) * POWER)
+    return (q - driving) / (closed + coef * jnp.abs(q) * power)
 
 
 def kernel(
     nx, ny, cap,
     depth_in, bed_in, east_in, south_in, rough_in, wet_in, soil_in, rain_in, col_in, blk_in,
-    h, qe, qs, newsoil,
+    h, qe, qs, dry, gain, mine, edge, from_row, from_col, at_end,
     bed, fric, rough, wet, land_in, index,
     tile_face, rim, rim_face, flank, flank_face,
     give, take, give_idx, take_idx, give_lev, take_lev,
     st_rows, st_cols, st_corner, st_in_rows, st_in_cols, st_in_corner,
     h_rows, h_cols, h_in_rows, h_in_cols, h_in_corner,
-    place, place_t, where_to, where_to_t, from_row, from_col, at_end, give_edge, take_edge, span,
+    place, place_t, where_to, where_to_t, give_edge, take_edge, span,
     in_sem, give_r, lev_r, edge_r, data_s, idx_s, idx_r, st_s, st_r, hs_s, hs_r,
 ):
     gx, gy = lax.axis_index("gx"), lax.axis_index("gy")
@@ -198,6 +202,9 @@
     take_idx[0] = give_idx[0]
 
     settle(in_sem.at[2], 5 * tr * tc // (EDGE * LANES))
+    bed[...] = bed[...] * DEEP
+    qe[...] = qe[...] * FLOW
+    qs[...] = qs[...] * FLOW
     kind = rough[...]
     f = jnp.zeros((tr, tc), jnp.float32)
     for i, coefficient in enumerate(MANNING):
@@ -276,7 +283,6 @@
         st_piece, (2 * chunks, 2 * (tr // LANES), 1), st_s, st_r
     )
     h_start, h_wait, h_done = edges(h_piece, (chunks, tr // LANES, 1), hs_s, hs_r)
-    st_start()
 
     lane = lax.broadcasted_iota(jnp.int32, (tr, LANES), 1)
     own = lane < LANES // 2
@@ -292,20 +298,21 @@
 
     def faces(b, fr, out):
         b_e, f_e, b_s, f_s = east_of(b), east_of(fr), south_of(b), south_of(fr)
-        half = 0.5 * GRAVITY * TIME_STEP
         out[0] = jnp.maximum(b, b_e)
         out[1] = jnp.maximum(b, b_s)
-        out[2] = jnp.where((fr > 0.0) & (f_e > 0.0), half * (fr + f_e), -1.0)
-        out[3] = jnp.where((fr > 0.0) & (f_s > 0.0), half * (fr + f_s), -1.0)
-
-    def substep(depth, b, e, s, out):
-        eta = depth + b
-        e = face(eta, east_of(eta), out[0], out[2], e)
-        s = face(eta, south_of(eta), out[1], out[3], s)
-        depth = depth + (TIME_STEP / CELL_WIDTH) * (
-            pltpu.roll(e, 1, 1) - e + pltpu.roll(s, 1, 0) - s
-        )
-        return depth, e, s
+        for i, other in ((2, f_e), (3, f_s)):
+            is_open = (fr > 0.0) & (other > 0.0)
+            out[i] = jnp.where(is_open, DRAG * (fr + other), 0.0)
+            out[i + 2] = jnp.where(is_open, 1.0, jnp.inf)
+
+    def substep(step, h, b, e, s, out):
+        eta = h[...] + b[...] if step == 0 else h[...]
+        east = face(eta, east_of(eta), out[0], out[2], out[4], e[...])
+        south = face(eta, south_of(eta), out[1], out[3], out[5], s[...])
+        e[...] = east
+        s[...] = south
+        eta = eta + (pltpu.roll(east, 1, 1) - east + pltpu.roll(south, 1, 0) - south)
+        h[...] = eta - b[...] if step == SUB - 1 else eta
 
     for i, x in enumerate((bed, fric, qe, qs)):
         keep(x, i)
@@ -327,7 +334,7 @@
     head, tail = chunk == 0.0, chunk == chunks - 1.0
     key = jnp.where((head | tail) & jnp.logical_not(outer), row, -1.0)
     for k in range(ny):
-        from_col[k] = one_hot(tr, jnp.where(turn_of == k, key, -1.0))
+        from_col[:, k * tr : (k + 1) * tr] = one_hot(tr, jnp.where(turn_of == k, key, -1.0))
     line = lax.broadcasted_iota(jnp.int32, (LANES, land), 0)
     ends = ((line < reach) & head) | ((line >= LANES - reach) & tail)
     at_end[...] = ends.astype(jnp.float32).T
@@ -345,13 +352,16 @@
         where_to_t[d] = target.T.astype(jnp.bfloat16)
 
     pltpu.make_async_copy(depth_in, h, in_sem.at[3]).wait()
+    h[...] = h[...] * DEEP
     inflow = pick(where_to[0], give[0])
     for k in offsets(ny):
+        if k == offsets(ny)[-1]:
+            st_start()
         arrive(take.at[k], give_r.at[k - 1])
         inflow = inflow + pick(where_to[k], take[k])
     for c in range(chunks):
         at = (pl.ds(0, tr), pl.ds(c * LANES, LANES))
-        h[at] = h[at] + inflow[c * tr : (c + 1) * tr]
+        h[at] = h[at] + DEEP * inflow[c * tr : (c + 1) * tr]
 
     h_rows[0] = h[0:EDGE, 0:tc]
     h_rows[1] = h[tr - EDGE : tr, 0:tc]
@@ -360,7 +370,7 @@
     keep(h, 4)
 
     for step in range(SUB):
-        h[...], qe[...], qs[...] = substep(h[...], bed[...], qe[...], qs[...], tile_face)
+        substep(step, h, bed, qe, qs, tile_face)
 
     high = lax.broadcasted_iota(jnp.int32, (tr, LANES), 0)
     within = (high >= reach) & (high < tr - reach)
@@ -373,7 +383,7 @@
             inside = inside & (lane < LANES - reach)
         blocks.append(jnp.where(inside, h[:, c * LANES : (c + 1) * LANES], 0.0))
     blocks = split(jnp.concatenate(blocks, axis=0))
-    for k in offsets(ny):
+    for k in offsets(ny)[::-1]:
         give_lev[k] = pick(where_to_t[k], blocks)
         send(give_lev.at[k], take_lev.at[k], data_s, lev_r.at[k - 1], from_peer(k))
     take_lev[0] = pick(where_to_t[0], blocks)
@@ -420,7 +430,7 @@
 
     for step in range(SUB):
         for x, out in ((rim, rim_face), (flank, flank_face)):
-            x[4], x[2], x[3] = substep(x[4], x[0], x[2], x[3], out)
+            substep(step, x.at[4], x.at[0], x.at[2], x.at[3], out)
 
     def merge(i, x):
         x[0:EDGE] = jnp.where(sub_low, rim[i, 2 * EDGE : 3 * EDGE], x[0:EDGE])
@@ -440,27 +450,20 @@
     take_edge[0] = give_edge[...]
     merge(2, qe)
     merge(3, qs)
-    mine = pick(place_t[0], take_lev[0])
-    for k in offsets(ny):
+    h[...] = h[...] * (1.0 / DEEP)
+    qe[...] = qe[...] * (1.0 / FLOW)
+    qs[...] = qs[...] * (1.0 / FLOW)
+    store, rain = land_in[0], land_in[1]
+    dry[...] = store + rain - rain * store * store
+    gain[...] = INFIL_RATE * (1.0 - store)
+    levels = pick(place_t[0], take_lev[0])
+    for k in offsets(ny)[::-1]:
         arrive(take_lev.at[k], lev_r.at[k - 1])
-        mine = mine + pick(place_t[k], take_lev[k])
+        levels = levels + pick(place_t[k], take_lev[k])
+    mine[...] = levels
     if ny > 1:
         arrive(take_edge.at[pl.ds(1, ny - 1)], edge_r)
-    table = [
-        take_edge[k, :, c * LANES : (c + 1) * LANES] for k in range(ny) for c in range(chunks)
-    ]
-    mine = mine + pick(from_row[...], jnp.concatenate(table, axis=0))
-    blank = jnp.zeros((LANES - 2 * EDGE, tr), jnp.float32)
-    sides = jnp.zeros((land, LANES), jnp.float32)
-    for k in range(ny):
-        side = take_edge[k, :, tc : tc + tr]
-        sides = sides + pick(from_col[k], jnp.concatenate([side, blank, side], axis=0).T)
-    mine = mine + at_end[...] * sides
-    store, rain = land_in[0], land_in[1]
-    runoff = rain * store * store
-    newsoil[...] = (
-        store + rain - runoff + INFIL_RATE * (1.0 - store) * (1.0 - jnp.exp(-mine))
-    )
+    edge[...] = take_edge[...]
     if ny > 1:
         arrive(settle_idx, idx_s)
         settle(data_s, (ny - 1) * (2 * cap // EDGE + (tc + tr) // LANES))
@@ -468,17 +471,31 @@
     h_done()
 
 
-def write_out(h, qe, qs, newsoil, depth_out, east_out, south_out, soil_out, sem):
+def finish(
+    h, qe, qs, dry, gain, mine, edge, from_row, from_col, at_end,
+    depth_out, east_out, south_out, soil_out,
+    newsoil, sem,
+):
+    ny, tr = edge.shape[0], h.shape[0]
+    chunks = h.shape[1] // LANES
     copies = [
         pltpu.make_async_copy(src, dst, sem.at[i])
         for i, (src, dst) in enumerate(
-            [
-                (h, depth_out), (qe, east_out), (qs, south_out), (newsoil, soil_out),
-            ]
+            [(h, depth_out), (qe, east_out), (qs, south_out), (newsoil, soil_out)]
         )
     ]
-    for c in copies:
+    for c in copies[:-1]:
         c.start()
+    table = [edge[k, :, c * LANES : (c + 1) * LANES] for k in range(ny) for c in range(chunks)]
+    levels = mine[...] + pick(from_row[...], jnp.concatenate(table, axis=0))
+    blank = jnp.zeros((LANES - 2 * EDGE, tr), jnp.float32)
+    sides = []
+    for k in range(ny):
+        side = edge[k, :, chunks * LANES :]
+        sides.append(jnp.concatenate([side, blank, side], axis=0).T)
+    levels = levels + at_end[...] * pick(from_col[...], jnp.concatenate(sides, axis=0))
+    newsoil[...] = dry[...] + gain[...] * (1.0 - jnp.exp(levels * (-1.0 / DEEP)))
+    copies[-1].start()
     for c in copies:
         c.wait()
 
@@ -506,14 +523,18 @@
     shape = jax.ShapeDtypeStruct
     out = pl.pallas_call(
         functools.partial(kernel, nx, ny, cap),
-        out_shape=[shape(grid, f32)] * 3 + [shape((land, LANES), f32)],
+        out_shape=[shape(grid, f32)] * 3
+        + [shape((land, LANES), f32)] * 3
+        + [shape((ny, EDGE, tc + tr), f32)]
+        + [shape((land, ny * (tc // LANES) * EDGE), bf16), shape((land, ny * tr), bf16)]
+        + [shape((land, LANES), f32)],
         in_specs=[any_] * 10,
-        out_specs=[vmem] * 4,
+        out_specs=[vmem] * 10,
         scratch_shapes=[v(grid, f32)] * 2
         + [v((tr, tc), i32)] * 2
         + [v((2, land, LANES), f32), v((2, 1, land), i32)]
-        + [v((4, *grid), f32), v((5, *rim), f32), v((4, *rim), f32)]
-        + [v((5, *flank), f32), v((4, *flank), f32)]
+        + [v((6, *grid), f32), v((5, *rim), f32), v((6, *rim), f32)]
+        + [v((5, *flank), f32), v((6, *flank), f32)]
         + [v((ny, cap, LANES), f32)] * 2
         + [v((ny, 1, cap), f32)] * 2
         + [v((ny, cap, LANES), f32)] * 2
@@ -521,7 +542,6 @@
         + edge_bufs(()) + edge_bufs(()) + [in_corners]
         + [v((ny, cap, land), bf16), v((ny, land, cap), bf16)]
         + [v((ny, land, cap), bf16), v((ny, cap, land), bf16)]
-        + [v((land, ny * (tc // LANES) * EDGE), bf16), v((ny, land, tr), bf16), v((land, LANES), f32)]
         + [v((EDGE, tc + tr), f32), v((ny, EDGE, tc + tr), f32)]
         + [v((span // (EDGE * LANES), EDGE, LANES), f32)]
         + [dma((4,))]
@@ -539,12 +559,12 @@
         )
     )
     out = pl.pallas_call(
-        write_out,
+        finish,
         out_shape=[shape((tr, tc), f32)] * 3 + [shape((land, LANES), f32)],
-        in_specs=[vmem] * 4,
+        in_specs=[vmem] * 10,
         out_specs=[any_] * 4,
-        scratch_shapes=[dma((4,))],
-        compiler_params=pltpu.CompilerParams(vmem_limit_bytes=8 << 20),
+        scratch_shapes=[v((land, LANES), f32), dma((4,))],
+        compiler_params=pltpu.CompilerParams(vmem_limit_bytes=16 << 20),
     )(*out)
     return out[0], out[1], out[2], out[3][None]
 

time: 22.7 us -> 21.6 us (0.952)
  Pallas kernels: 21.9 us -> 20.8 us
    pallas_call x1, Pallas kernels: 21 us -> 19.7 us  [local(): pl.pallas_call(functools.partial(kernel, nx, ny, cap), out_shape=[shape(g...]
where the time goes in v3:
time: 21.6 us; the launch traced here: 21.5 us
  Pallas kernels  20.8 us (96%)
  between operations  0.64 us (3%)
    pallas_call x1, Pallas kernels, local(): pl.pallas_call(functools.partial(kernel, nx, ny, cap), out_shape=[shape(g...  19.7 us
    pallas_call x1, Pallas kernels, local(): pl.pallas_call(finish, out_shape=[shape((tr, tc), f32)] * 3 + [shape((lan...  1.13 us

profile of v3, /device:TPU:0, one launch (start us, length us, event | category | flops | bytes accessed | tf_op | source)
XLA Modules:
  0.0 21.5 jit_solution(14961120570087452067)
XLA Ops:
  0.6 19.7 %shard_map.129 = (f32[128,384]{1,0:T(8,128)S(1)}, f32[128,384]{1,0:T(8,128)S(1)}, f32[128,384]{1,0:T(8,128)S(1)}, f32[384,128]{1,0:T(8,128)S(1)}, f32[384,128]{1...) custom-call(f32[128,384]{1,0:T(8,128)} %depth_in.1, ...), custom_call_target="tpu_custom_call" | custom-call | tf_op jit(solution)/shard_map/pallas_call | solution.py:524
  20.3 1.1 %shard_map.130 = (f32[128,384]{1,0:T(8,128)}, f32[128,384]{1,0:T(8,128)}, f32[128,384]{1,0:T(8,128)}, f32[384,128]{1,0:T(8,128)}) custom-call(f32[128,384]{1,0:T(8,128)S(1)} %get-tuple-element.18.h, f32[128,384]{1,0:T(8,128)S(1)} %get-tuple-element.19.qe, f32[128,384]{1,0:T(8,128)S(1)} %get-tuple-element.20.qs, f32[384,128]{1,0:T(8,128)S(1)} %get-tuple-element.21.dry, ...), custom_call_target="tpu_custom_call" | custom-call | tf_op jit(solution)/shard_map/pallas_call | solution.py:561
